TPU v7x, 256 devices: a whole 4x4x8 slice. The times are simulated.
256 devices in a mesh: section: 16 (over x_hi, y, core), tm: 16 (over z, x_lo).
Axes of the slice: x: 4 (x_hi: 2, x_lo: 2; x = x_hi * 2 + x_lo), y: 4, z: 8, core: 2. Of those that a mesh axis runs over, the one named last changes fastest.
Arguments:
- fwd_input: bfloat16 [16, 2048, 1536], P('section', 'tm'), may hold values from -6 to 6
- saved_input: bfloat16 [16, 2048, 1536], P('section', 'tm'), may hold values from -6 to 6
- grad_in: bfloat16 [16, 2048, 1536], P('section', 'tm'), may hold values from -6 to 6
- gain: float32 [16, 1536], P('section'), may hold values from 0.25 to 1.75
- kernel: float32 [16, 31, 1536], P('section'), may hold values from -1 to 1
- w_out: bfloat16 [16, 1536, 1536], P('section', 'tm'), may hold values from -0.15625 to 0.15625
- lengths: int32 [32], replicated, may hold values from 1 to 2048, 49152 in all
- plan: int32 [16, 2], P('section'), may hold values from 0 to 31
Outputs:
- passed_activation: bfloat16 [16, 2048, 1536], P('section', 'tm')
- passed_gradient: bfloat16 [16, 2048, 1536], P('section', 'tm')
- weight_grad: float32 [16, 1536, 1536], P('section', 'tm')
- kernel_grad: float32 [16, 31, 1536], P('section')
- gain_grad: float32 [16, 1536], P('section')
Inputs may be any that keep to these rules, and one draw needn't show every extreme that they name: `lengths`: 32 valid counts summing to 49152, the largest exactly 2048. `plan`: indices into lengths.
All inputs are finite; a program needn't handle non-finite values.
Results may differ from a plain program's by a relative error of at most 0.017.
Values may be sent and summed in bfloat16 or wider, within the bound.
No kernel may reach another device: no remote copies, remote signals or barrier semaphores. Data moves between devices by JAX's collectives and lax.ppermute only.
A program may use at most 64 MiB of HBM per device.

v0:
```python
import jax
import jax.numpy as jnp
from jax import lax
from jax.sharding import PartitionSpec as P

KW = 31


def extended(array, sides, width):
    for axis, dim in sides:
        size, length = (lax.axis_size(axis), array.shape[dim])
        up = [(i, (i + 1) % size) for i in range(size - 1)]
        down = [(j, i) for i, j in up]
        last = lax.slice_in_dim(array, length - width, length, axis=dim)
        first = lax.slice_in_dim(array, 0, width, axis=dim)
        before = lax.ppermute(last, axis, up)
        after = lax.ppermute(first, axis, down)
        array = jnp.concatenate([before, array, after], axis=dim)
    return array


def from_behind(array, axis, by):
    length = lax.axis_size(axis)
    pairs = [(i, i + by) for i in range(length) if 0 <= i + by < length]
    return lax.ppermute(array, axis, pairs)


def normalize(values):
    center = values - jnp.mean(values, axis=-1, keepdims=True)
    inverse = lax.rsqrt(jnp.mean(center * center, axis=-1, keepdims=True) + 1e-05)
    return (center * inverse, inverse)


def swish_act(values):
    return values * jax.nn.sigmoid(values)


def conv_taps(padded, kernel_rows, frames):
    running = jnp.zeros(padded.shape[:-2] + (frames, padded.shape[-1]), jnp.float32)
    for tap_index in range(KW):
        running = running + kernel_rows[tap_index] * padded[..., tap_index : tap_index + frames, :]
    return running


def per_device(fwd_input, saved_input, grad_in, gain, kernel, w_out, lengths, plan):
    frames = fwd_input.shape[1]
    pieces = lax.axis_size("tm")
    margin = KW // 2
    factor = float(frames * pieces) ** (-0.5)
    position = lax.axis_index("tm") * frames + lax.iota(jnp.int32, frames)
    slot_ids = lax.iota(jnp.int32, lengths.shape[0])
    fwd_len = jnp.sum(jnp.where(slot_ids == plan[0, 0], lengths, 0))
    bwd_len = jnp.sum(jnp.where(slot_ids == plan[0, 1], lengths, 0))
    fwd_mask = (position < fwd_len).astype(jnp.float32)[:, None]
    bwd_mask = (position < bwd_len).astype(jnp.float32)[:, None]
    gain_row = gain[0]
    kernel_rows = kernel[0]
    w_rows = w_out[0]
    upstream = grad_in[0]
    fwd_float = fwd_input[0].astype(jnp.float32)
    fwd_hat, unused_inverse = normalize(fwd_float)
    saved_hat, inverse = normalize(saved_input[0].astype(jnp.float32))
    conv_fwd = (fwd_hat * gain_row * fwd_mask).astype(jnp.bfloat16)
    conv_saved = (saved_hat * gain_row * bwd_mask).astype(jnp.bfloat16)
    padded = extended(jnp.stack([conv_fwd, conv_saved]), (("tm", 1),), margin)
    padded_float = padded.astype(jnp.float32)
    mixed_all = conv_taps(padded_float, kernel_rows, frames)
    mixed_saved = mixed_all[1]
    hidden_fwd = swish_act(mixed_all[0]).astype(jnp.bfloat16)
    hidden_saved = swish_act(mixed_saved).astype(jnp.bfloat16)
    columns = hidden_fwd
    product = jnp.dot(
        columns,
        lax.all_gather(w_rows, "tm", axis=0, tiled=True),
        preferred_element_type=jnp.float32,
    )
    hidden_grad = lax.dot_general(
        upstream,
        lax.all_gather(w_rows, "tm", axis=0, tiled=True),
        (((1,), (1,)), ((), ())),
        preferred_element_type=jnp.float32,
    )
    output = (fwd_float + product).astype(jnp.bfloat16)
    passed_activation = from_behind(output[None], "section", 1)
    gate_sig = jax.nn.sigmoid(mixed_saved)
    conv_grad = (hidden_grad * (gate_sig + mixed_saved * gate_sig * (1.0 - gate_sig))).astype(
        jnp.bfloat16
    )
    pad_grad = extended(conv_grad, (("tm", 0),), margin).astype(jnp.float32)
    input_grad = jnp.zeros((frames, conv_grad.shape[1]), jnp.float32)
    for tap_index in range(KW):
        begin_at = 2 * margin - tap_index
        input_grad = input_grad + kernel_rows[tap_index] * pad_grad[begin_at : begin_at + frames]
    grad_float = conv_grad.astype(jnp.float32)
    pad_saved = padded_float[1]
    kernel_local = (
        jnp.stack(
            [
                jnp.sum(grad_float * pad_saved[tap_index : tap_index + frames], axis=0)
                for tap_index in range(KW)
            ]
        )
        * factor
    )
    norm_grad = input_grad * bwd_mask
    gain_local = jnp.sum(norm_grad * saved_hat, axis=0) * factor
    kernel_grad, gain_grad = (
        lax.psum(kernel_local.astype(jnp.bfloat16), "tm").astype(jnp.float32),
        lax.psum(gain_local.astype(jnp.bfloat16), "tm").astype(jnp.float32),
    )
    columns = hidden_saved
    partial_value = (
        lax.dot_general(
            columns, upstream, (((0,), (0,)), ((), ())), preferred_element_type=jnp.float32
        )
        * factor
    )
    weight_grad = lax.psum_scatter(
        lax.optimization_barrier(partial_value.astype(jnp.bfloat16))
        .astype(jnp.float32)
        .astype(jnp.bfloat16),
        "tm",
        scatter_dimension=0,
        tiled=True,
    ).astype(jnp.float32)
    hat_grad = norm_grad * gain_row
    input_back = upstream.astype(jnp.float32) + inverse * (
        hat_grad
        - jnp.mean(hat_grad, axis=-1, keepdims=True)
        - saved_hat * jnp.mean(hat_grad * saved_hat, axis=-1, keepdims=True)
    )
    passed_gradient = from_behind(input_back.astype(jnp.bfloat16)[None], "section", -1)
    return (
        passed_activation,
        passed_gradient,
        weight_grad[None],
        kernel_grad[None],
        gain_grad[None],
    )


def solution(mesh):
    placed = (
        P("section", "tm", None),
        P("section", "tm", None),
        P("section", "tm", None),
        P("section", None),
        P("section", None, None),
        P("section", "tm", None),
        P(),
        P("section", None),
    )
    return jax.shard_map(
        per_device,
        mesh=mesh,
        in_specs=placed,
        out_specs=(
            P("section", "tm", None),
            P("section", "tm", None),
            P("section", "tm", None),
            P("section", None, None),
            P("section", None),
        ),
        check_vma=False,
    )
```

profile of v0, /device:TPU:42, one launch (start us, length us, event | category | flops | bytes accessed | tf_op | source)
XLA Modules:
  0.0 398.9 jit_solution(7578486727265539355)
XLA Ops:
  7.2 0.0 copy-start.1
  7.2 0.0 copy-start
  7.2 0.0 all-gather.3.cloned.1.call-start
  7.2 0.7 all-gather.3.cloned.1.call-update
  7.9 0.0 all-reduce.2.cloned.1.call-start
  8.0 0.7 reduce.3
  8.7 1.3 fusion.152
  10.0 2.6 fusion.146
  12.6 1.3 compare_convert_fusion
  13.9 0.0 copy-start.69
  13.9 1.1 convert_reduce_fusion.1
  15.0 1.1 convert_reduce_fusion
  16.2 1.2 fusion.52
  17.5 0.3 fusion.73
  17.7 0.4 fusion.56
  18.2 3.8 collective-permute-start
  22.0 2.0 collective-permute-start.1
  24.1 0.3 slice_reduce_fusion.30
  24.6 0.2 slice_reduce_fusion.29
  24.9 0.0 copy-start.61
  24.9 0.0 copy-start.63
  24.9 0.6 collective-permute-done
  25.5 6.0 %collective-permute-done.1 = bf16[2,15,1536]{2,1,0:T(8,128)(2,1)S(1)} collective-permute-done((bf16[2,15,1536]{2,1,0:T(8,128)(2,1)S(1)}, bf16[2,15,1536]{2,1,0:T(8,128)(2,1)S(1)}, u32[]{:S(2)}, u32[]{:S(2)}) %collective-permute-start.1) | collective-permute-done | bytes 92192 | tf_op jit(solution)/shard_map/ppermute | solution.py:17
  31.5 0.3 maximum_convert_fusion
  32.1 0.0 copy-start.3
  32.1 6.8 %fusion.20 = f32[2,128,1536]{2,1,0:T(8,128)} fusion(f32[2,158,1536]{2,1,0:T(8,128)S(1)} %maximum_convert_fusion, f32[1536]{0:T(1024)S(1)} %get-tuple-element.68, f32[1536]{0:T(1024)S(1)} %get-tuple-element.69, f32[1536]{0:T(1024)S(1)} %get-tuple-element.40, f32[1536]{0:T(1024)S(1)} %get-tuple-element.41, f32[1536]{0:T(1024)S(1)} %get-tuple-element.42, ...), kind=kLoop, calls=%fused_computation.43 | loop fusion | flops 23986176 | bytes 50522112 | tf_op jit(solution)/shard_map/add | solution.py:41
  38.9 86.8 %all-gather.3.cloned.1.call-done = bf16[1,1536,1536]{2,1,0:T(8,128)(2,1)} async-done(((bf16[1,96,1536]{2,1,0:T(8,128)(2,1)}), bf16[1,1536,1536]{2,1,0:T(8,128)(2,1)}) %all-gather.3.cloned.1.call-update) | async-done | bytes 4718608 | tf_op jit(solution)/shard_map/all_gather | solution.py:74
  125.8 5.5 %fusion.103 = (f32[1536]{0:T(1024)S(1)}, f32[1536]{0:T(1024)S(1)}, f32[1536]{0:T(1024)S(1)}, f32[1536]{0:T(1024)S(1)}, f32[1536]{0:T(1024)S(1)}, /*index=5*/f32[...) fusion(f32[2,158,1536]{2,1,0:T(8,128)S(1)} %maximum_convert_fus, ...), kind=kOutput, calls=%fused_computation.163 | convolution fusion | flops 611037696 | bytes 16594944 | tf_op jit(solution)/shard_map/dot_general | solution.py:77
  131.2 2.0 fusion.104
  133.6 0.6 stack.113
  134.2 0.6 stack.114
  134.8 0.6 stack.115
  135.4 0.6 stack.116
  136.0 0.6 stack.117
  136.6 0.6 stack.118
  137.2 0.6 stack.119
  137.8 1.8 stack.133
  139.6 0.8 broadcast_in_dim.42
  140.3 0.0 all-reduce.2.cloned.1.call-update
  140.4 0.0 reduce-scatter.2.cloned.1.call-start
  140.4 3.6 fusion
  144.0 0.0 reduce-scatter.2.cloned.1.call-update
  144.1 2.4 collective-permute-start.3
  146.8 0.0 copy-start.62
  146.8 0.0 copy-start.64
  146.9 3.5 collective-permute-start.4
  150.4 3.9 fusion.17
  154.3 2.1 collective-permute-start.2
  156.4 0.0 collective-permute-done.3
  156.4 0.0 collective-permute-done.4
  156.4 0.1 maximum_convert_fusion.1
  156.9 5.1 %fusion.72 = (f32[1536]{0:T(1024)S(1)}, f32[128]{0:T(128)S(1)}, f32[128]{0:T(128)S(1)}, f32[128,1536]{1,0:T(8,128)S(1)}) fusion(bf16[1,128,1536]{2,1,0:T(8,128)(2,1)S(1)} %copy-done, f32[128]{0:T(128)S(1)} %copy-done.68, f32[128]{0:T(128)S(1)} %copy-done.66, f32[1536]{0:T(1024)S(1)} %reduce.3, f32[128]{0:T(128)S(1)} %copy-done.70, ...), kind=kLoop, calls=%fused_computation.132 | loop fusion | flops 13957376 | bytes 25764352 | tf_op jit(solution)/shard_map/reduce_sum | solution.py:106
  162.0 0.4 fusion.141
  162.4 3.6 collective-permute-start.5
  166.1 31.3 %psum.15 = bf16[1,1536]{1,0:T(2,128)(2,1)S(1)} all-reduce(bf16[1,1536]{1,0:T(2,128)(2,1)S(1)} %broadcast_in_dim.44), channel_id=1, replica_groups=mesh['section'=16,'tm'=16] {'tm'}, use_global_device_ids=true, to_apply=%region_42.43 | all-reduce | flops 1536 | bytes 6144 | tf_op jit(solution)/shard_map/psum | solution.py:109
  197.4 0.6 broadcast_in_dim.45
  198.0 78.2 %all-reduce.2.cloned.1.call-done = bf16[1,31,1536]{2,0,1:T(2,128)(2,1)} async-done(((bf16[1,31,1536]{2,0,1:T(2,128)(2,1)}), bf16[1,31,1536]{2,0,1:T(2,128)(2,1)}) %all-reduce.2.cloned.1.call-update) | async-done | bytes 95248 | tf_op jit(solution)/shard_map/psum | solution.py:108
  276.2 1.8 broadcast_in_dim.43
  278.0 0.0 collective-permute-done.2
  278.0 0.0 collective-permute-done.5
  278.0 111.0 %reduce-scatter.2.cloned.1.call-done = bf16[96,1536]{1,0:T(8,128)(2,1)} async-done(((bf16[1536,1536]{1,0:T(8,128)(2,1)}), bf16[96,1536]{1,0:T(8,128)(2,1)}) %reduce-scatter.2.cloned.1.call-update) | async-done | bytes 294928 | tf_op jit(solution)/shard_map/reduce_scatter | solution.py:118
  389.0 1.8 bitcast_convert_fusion
  390.9 0.7 copy.16
  391.6 0.7 copy.17
  (168 shorter events, 0.5 us)
Async XLA Ops:
  7.2 10.6 %copy-start.1 = (bf16[1,128,1536]{2,1,0:T(8,128)(2,1)S(1)}, bf16[1,128,1536]{2,1,0:T(8,128)(2,1)}, u32[]{:S(2)}) copy-start(bf16[1,128,1536]{2,1,0:T(8,128)(2,1)} %param.8) | copy-start | bytes 1179652
  7.2 10.3 %copy-start = (bf16[1,128,1536]{2,1,0:T(8,128)(2,1)S(1)}, bf16[1,128,1536]{2,1,0:T(8,128)(2,1)}, u32[]{:S(2)}) copy-start(bf16[1,128,1536]{2,1,0:T(8,128)(2,1)} %param.9) | copy-start | bytes 1179652
  7.2 118.6 %all-gather.3.cloned.1.call-start = ((), (), s32[]{:S(2)}) async-start(), calls=%async_computation.3 | async-start | bytes 5013504 | tf_op jit(solution)/shard_map/all_gather | solution.py:74
  7.9 268.3 %all-reduce.2.cloned.1.call-start = ((), (), s32[]{:S(2)}) async-start(), calls=%async_computation.2 | async-start | bytes 380928 | tf_op jit(solution)/shard_map/psum | solution.py:108
  17.7 7.8 %copy-start.67 = (f32[128]{0:T(128)}, f32[128]{0:T(128)S(1)}, u32[]{:S(2)}) copy-start(f32[128]{0:T(128)S(1)} %get-tuple-element.84) | copy-start | bytes 1540
  18.2 7.3 %collective-permute-start = (bf16[2,15,1536]{2,1,0:T(8,128)(2,1)S(1)}, bf16[2,15,1536]{2,1,0:T(8,128)(2,1)S(1)}, u32[]{:S(2)}, u32[]{:S(2)}) collective-permute-start(bf16[2,15,1536]{2,1,0:T(8,128)(2,1)S(1)} %get-tuple-element.73), channel_id=1, source_target_pairs={{0,1},{1,2},{2,3},{3,4},{4,5},{5,6},{6,7},{7,8},{8,9},{9,10},{10,1... | collective-permute-start | bytes 276488 | tf_op jit(solution)/shard_map/ppermute | solution.py:16
  22.0 9.5 %collective-permute-start.1 = (bf16[2,15,1536]{2,1,0:T(8,128)(2,1)S(1)}, bf16[2,15,1536]{2,1,0:T(8,128)(2,1)S(1)}, u32[]{:S(2)}, u32[]{:S(2)}) collective-permute-start(bf16[2,15,1536]{2,1,0:T(8,128)(2,1)S(1)} %get-tuple-element.74), channel_id=1, source_target_pairs={{1,0},{2,1},{3,2},{4,3},{5,4},{6,5},{7,6},{8,7},{9,8},{10,9},{11,1... | collective-permute-start | bytes 276488 | tf_op jit(solution)/shard_map/ppermute | solution.py:17
  24.4 7.4 %copy-start.5 = (f32[1536]{0:T(1024)}, f32[1536]{0:T(1024)S(1)}, u32[]{:S(2)}) copy-start(f32[1536]{0:T(1024)S(1)} %get-tuple-element.40) | copy-start | bytes 18436
  24.4 7.4 %copy-start.7 = (f32[1536]{0:T(1024)}, f32[1536]{0:T(1024)S(1)}, u32[]{:S(2)}) copy-start(f32[1536]{0:T(1024)S(1)} %get-tuple-element.41) | copy-start | bytes 18436
  24.4 7.4 %copy-start.9 = (f32[1536]{0:T(1024)}, f32[1536]{0:T(1024)S(1)}, u32[]{:S(2)}) copy-start(f32[1536]{0:T(1024)S(1)} %get-tuple-element.42) | copy-start | bytes 18436
  24.4 7.4 %copy-start.11 = (f32[1536]{0:T(1024)}, f32[1536]{0:T(1024)S(1)}, u32[]{:S(2)}) copy-start(f32[1536]{0:T(1024)S(1)} %get-tuple-element.43) | copy-start | bytes 18436
  24.4 7.4 %copy-start.13 = (f32[1536]{0:T(1024)}, f32[1536]{0:T(1024)S(1)}, u32[]{:S(2)}) copy-start(f32[1536]{0:T(1024)S(1)} %get-tuple-element.44) | copy-start | bytes 18436
  24.4 7.4 %copy-start.15 = (f32[1536]{0:T(1024)}, f32[1536]{0:T(1024)S(1)}, u32[]{:S(2)}) copy-start(f32[1536]{0:T(1024)S(1)} %get-tuple-element.45) | copy-start | bytes 18436
  24.4 7.4 %copy-start.17 = (f32[1536]{0:T(1024)}, f32[1536]{0:T(1024)S(1)}, u32[]{:S(2)}) copy-start(f32[1536]{0:T(1024)S(1)} %get-tuple-element.46) | copy-start | bytes 18436
  24.4 7.4 %copy-start.19 = (f32[1536]{0:T(1024)}, f32[1536]{0:T(1024)S(1)}, u32[]{:S(2)}) copy-start(f32[1536]{0:T(1024)S(1)} %get-tuple-element.47) | copy-start | bytes 18436
  24.5 7.4 %copy-start.21 = (f32[1536]{0:T(1024)}, f32[1536]{0:T(1024)S(1)}, u32[]{:S(2)}) copy-start(f32[1536]{0:T(1024)S(1)} %get-tuple-element.48) | copy-start | bytes 18436
  24.5 7.4 %copy-start.23 = (f32[1536]{0:T(1024)}, f32[1536]{0:T(1024)S(1)}, u32[]{:S(2)}) copy-start(f32[1536]{0:T(1024)S(1)} %get-tuple-element.49) | copy-start | bytes 18436
  24.5 7.4 %copy-start.25 = (f32[1536]{0:T(1024)}, f32[1536]{0:T(1024)S(1)}, u32[]{:S(2)}) copy-start(f32[1536]{0:T(1024)S(1)} %get-tuple-element.50) | copy-start | bytes 18436
  24.5 7.4 %copy-start.27 = (f32[1536]{0:T(1024)}, f32[1536]{0:T(1024)S(1)}, u32[]{:S(2)}) copy-start(f32[1536]{0:T(1024)S(1)} %get-tuple-element.51) | copy-start | bytes 18436
  24.5 7.4 %copy-start.29 = (f32[1536]{0:T(1024)}, f32[1536]{0:T(1024)S(1)}, u32[]{:S(2)}) copy-start(f32[1536]{0:T(1024)S(1)} %get-tuple-element.52) | copy-start | bytes 18436
  24.5 7.4 %copy-start.31 = (f32[1536]{0:T(1024)}, f32[1536]{0:T(1024)S(1)}, u32[]{:S(2)}) copy-start(f32[1536]{0:T(1024)S(1)} %get-tuple-element.53) | copy-start | bytes 18436
  24.5 7.4 %copy-start.33 = (f32[1536]{0:T(1024)}, f32[1536]{0:T(1024)S(1)}, u32[]{:S(2)}) copy-start(f32[1536]{0:T(1024)S(1)} %get-tuple-element.54) | copy-start | bytes 18436
  24.5 7.4 %copy-start.35 = (f32[1536]{0:T(1024)}, f32[1536]{0:T(1024)S(1)}, u32[]{:S(2)}) copy-start(f32[1536]{0:T(1024)S(1)} %get-tuple-element.55) | copy-start | bytes 18436
  24.5 7.4 %copy-start.37 = (f32[1536]{0:T(1024)}, f32[1536]{0:T(1024)S(1)}, u32[]{:S(2)}) copy-start(f32[1536]{0:T(1024)S(1)} %get-tuple-element.56) | copy-start | bytes 18436
  24.5 7.4 %copy-start.39 = (f32[1536]{0:T(1024)}, f32[1536]{0:T(1024)S(1)}, u32[]{:S(2)}) copy-start(f32[1536]{0:T(1024)S(1)} %get-tuple-element.57) | copy-start | bytes 18436
  32.1 93.7 %copy-start.3 = (bf16[1,128,1536]{2,1,0:T(8,128)(2,1)S(1)}, bf16[1,128,1536]{2,1,0:T(8,128)(2,1)}, u32[]{:S(2)}) copy-start(bf16[1,128,1536]{2,1,0:T(8,128)(2,1)} %param.10) | copy-start | bytes 1179652
  140.4 248.7 %reduce-scatter.2.cloned.1.call-start = ((), (), s32[]{:S(2)}) async-start(), calls=%async_computation.1 | async-start | bytes 5013504 | tf_op jit(solution)/shard_map/reduce_scatter | solution.py:118
  144.1 12.3 %collective-permute-start.3 = (bf16[15,1536]{1,0:T(8,128)(2,1)S(1)}, bf16[15,1536]{1,0:T(8,128)(2,1)S(1)}, u32[]{:S(2)}, u32[]{:S(2)}) collective-permute-start(bf16[15,1536]{1,0:T(8,128)(2,1)S(1)} %get-tuple-element.75), channel_id=1, source_target_pairs={{0,1},{1,2},{2,3},{3,4},{4,5},{5,6},{6,7},{7,8},{8,9},{9,10},{10,1... | collective-permute-start | bytes 138248 | tf_op jit(solution)/shard_map/ppermute | solution.py:16
  146.5 10.0 %copy-start.6 = (f32[1536]{0:T(1024)S(1)}, f32[1536]{0:T(1024)}, u32[]{:S(2)}) copy-start(f32[1536]{0:T(1024)} %copy-done.5) | copy-start | bytes 18436
  146.5 10.0 %copy-start.8 = (f32[1536]{0:T(1024)S(1)}, f32[1536]{0:T(1024)}, u32[]{:S(2)}) copy-start(f32[1536]{0:T(1024)} %copy-done.7) | copy-start | bytes 18436
  146.6 10.0 %copy-start.10 = (f32[1536]{0:T(1024)S(1)}, f32[1536]{0:T(1024)}, u32[]{:S(2)}) copy-start(f32[1536]{0:T(1024)} %copy-done.9) | copy-start | bytes 18436
  146.6 10.0 %copy-start.12 = (f32[1536]{0:T(1024)S(1)}, f32[1536]{0:T(1024)}, u32[]{:S(2)}) copy-start(f32[1536]{0:T(1024)} %copy-done.11) | copy-start | bytes 18436
  146.6 10.0 %copy-start.14 = (f32[1536]{0:T(1024)S(1)}, f32[1536]{0:T(1024)}, u32[]{:S(2)}) copy-start(f32[1536]{0:T(1024)} %copy-done.13) | copy-start | bytes 18436
  146.6 10.0 %copy-start.16 = (f32[1536]{0:T(1024)S(1)}, f32[1536]{0:T(1024)}, u32[]{:S(2)}) copy-start(f32[1536]{0:T(1024)} %copy-done.15) | copy-start | bytes 18436
  146.6 10.0 %copy-start.18 = (f32[1536]{0:T(1024)S(1)}, f32[1536]{0:T(1024)}, u32[]{:S(2)}) copy-start(f32[1536]{0:T(1024)} %copy-done.17) | copy-start | bytes 18436
  146.6 10.0 %copy-start.20 = (f32[1536]{0:T(1024)S(1)}, f32[1536]{0:T(1024)}, u32[]{:S(2)}) copy-start(f32[1536]{0:T(1024)} %copy-done.19) | copy-start | bytes 18436
  146.6 10.0 %copy-start.22 = (f32[1536]{0:T(1024)S(1)}, f32[1536]{0:T(1024)}, u32[]{:S(2)}) copy-start(f32[1536]{0:T(1024)} %copy-done.21) | copy-start | bytes 18436
  146.6 10.0 %copy-start.24 = (f32[1536]{0:T(1024)S(1)}, f32[1536]{0:T(1024)}, u32[]{:S(2)}) copy-start(f32[1536]{0:T(1024)} %copy-done.23) | copy-start | bytes 18436
  146.6 10.0 %copy-start.26 = (f32[1536]{0:T(1024)S(1)}, f32[1536]{0:T(1024)}, u32[]{:S(2)}) copy-start(f32[1536]{0:T(1024)} %copy-done.25) | copy-start | bytes 18436
  146.6 10.0 %copy-start.28 = (f32[1536]{0:T(1024)S(1)}, f32[1536]{0:T(1024)}, u32[]{:S(2)}) copy-start(f32[1536]{0:T(1024)} %copy-done.27) | copy-start | bytes 18436
  146.7 10.0 %copy-start.30 = (f32[1536]{0:T(1024)S(1)}, f32[1536]{0:T(1024)}, u32[]{:S(2)}) copy-start(f32[1536]{0:T(1024)} %copy-done.29) | copy-start | bytes 18436
  146.7 10.0 %copy-start.32 = (f32[1536]{0:T(1024)S(1)}, f32[1536]{0:T(1024)}, u32[]{:S(2)}) copy-start(f32[1536]{0:T(1024)} %copy-done.31) | copy-start | bytes 18436
  146.7 10.0 %copy-start.34 = (f32[1536]{0:T(1024)S(1)}, f32[1536]{0:T(1024)}, u32[]{:S(2)}) copy-start(f32[1536]{0:T(1024)} %copy-done.33) | copy-start | bytes 18436
  146.7 10.0 %copy-start.36 = (f32[1536]{0:T(1024)S(1)}, f32[1536]{0:T(1024)}, u32[]{:S(2)}) copy-start(f32[1536]{0:T(1024)} %copy-done.35) | copy-start | bytes 18436
  146.7 10.0 %copy-start.38 = (f32[1536]{0:T(1024)S(1)}, f32[1536]{0:T(1024)}, u32[]{:S(2)}) copy-start(f32[1536]{0:T(1024)} %copy-done.37) | copy-start | bytes 18436
  146.7 10.0 %copy-start.40 = (f32[1536]{0:T(1024)S(1)}, f32[1536]{0:T(1024)}, u32[]{:S(2)}) copy-start(f32[1536]{0:T(1024)} %copy-done.39) | copy-start | bytes 18436
  146.7 10.0 %copy-start.42 = (f32[1536]{0:T(1024)S(1)}, f32[1536]{0:T(1024)}, u32[]{:S(2)}) copy-start(f32[1536]{0:T(1024)} %copy-done.41) | copy-start | bytes 18436
  146.7 10.0 %copy-start.44 = (f32[1536]{0:T(1024)S(1)}, f32[1536]{0:T(1024)}, u32[]{:S(2)}) copy-start(f32[1536]{0:T(1024)} %copy-done.43) | copy-start | bytes 18436
  146.7 10.0 %copy-start.46 = (f32[1536]{0:T(1024)S(1)}, f32[1536]{0:T(1024)}, u32[]{:S(2)}) copy-start(f32[1536]{0:T(1024)} %copy-done.45) | copy-start | bytes 18436
  146.7 10.0 %copy-start.48 = (f32[1536]{0:T(1024)S(1)}, f32[1536]{0:T(1024)}, u32[]{:S(2)}) copy-start(f32[1536]{0:T(1024)} %copy-done.47) | copy-start | bytes 18436
  146.8 10.0 %copy-start.50 = (f32[1536]{0:T(1024)S(1)}, f32[1536]{0:T(1024)}, u32[]{:S(2)}) copy-start(f32[1536]{0:T(1024)} %copy-done.49) | copy-start | bytes 18436
  146.8 10.0 %copy-start.52 = (f32[1536]{0:T(1024)S(1)}, f32[1536]{0:T(1024)}, u32[]{:S(2)}) copy-start(f32[1536]{0:T(1024)} %copy-done.51) | copy-start | bytes 18436
  146.8 10.0 %copy-start.54 = (f32[1536]{0:T(1024)S(1)}, f32[1536]{0:T(1024)}, u32[]{:S(2)}) copy-start(f32[1536]{0:T(1024)} %copy-done.53) | copy-start | bytes 18436
  146.8 10.0 %copy-start.56 = (f32[1536]{0:T(1024)S(1)}, f32[1536]{0:T(1024)}, u32[]{:S(2)}) copy-start(f32[1536]{0:T(1024)} %copy-done.55) | copy-start | bytes 18436
  146.8 10.0 %copy-start.58 = (f32[1536]{0:T(1024)S(1)}, f32[1536]{0:T(1024)}, u32[]{:S(2)}) copy-start(f32[1536]{0:T(1024)} %copy-done.57) | copy-start | bytes 18436
  146.8 10.0 %copy-start.60 = (f32[1536]{0:T(1024)S(1)}, f32[1536]{0:T(1024)}, u32[]{:S(2)}) copy-start(f32[1536]{0:T(1024)} %copy-done.59) | copy-start | bytes 18436
  146.8 10.0 %copy-start.62 = (f32[1536]{0:T(1024)S(1)}, f32[1536]{0:T(1024)}, u32[]{:S(2)}) copy-start(f32[1536]{0:T(1024)} %copy-done.61) | copy-start | bytes 18436
  146.8 10.0 %copy-start.64 = (f32[1536]{0:T(1024)S(1)}, f32[1536]{0:T(1024)}, u32[]{:S(2)}) copy-start(f32[1536]{0:T(1024)} %copy-done.63) | copy-start | bytes 18436
  146.8 10.0 %copy-start.66 = (f32[128]{0:T(128)S(1)}, f32[128]{0:T(128)}, u32[]{:S(2)}) copy-start(f32[128]{0:T(128)} %copy-done.65) | copy-start | bytes 1540
  146.8 10.0 %copy-start.68 = (f32[128]{0:T(128)S(1)}, f32[128]{0:T(128)}, u32[]{:S(2)}) copy-start(f32[128]{0:T(128)} %copy-done.67) | copy-start | bytes 1540
  146.9 10.0 %copy-start.70 = (f32[128]{0:T(128)S(1)}, f32[128]{0:T(128)}, u32[]{:S(2)}) copy-start(f32[128]{0:T(128)} %copy-done.69) | copy-start | bytes 1540
  146.9 9.6 %collective-permute-start.4 = (bf16[15,1536]{1,0:T(8,128)(2,1)S(1)}, bf16[15,1536]{1,0:T(8,128)(2,1)S(1)}, u32[]{:S(2)}, u32[]{:S(2)}) collective-permute-start(bf16[15,1536]{1,0:T(8,128)(2,1)S(1)} %get-tuple-element.76), channel_id=1, source_target_pairs={{1,0},{2,1},{3,2},{4,3},{5,4},{6,5},{7,6},{8,7},{9,8},{10,9},{11,1... | collective-permute-start | bytes 138248 | tf_op jit(solution)/shard_map/ppermute | solution.py:17
  154.3 123.7 %collective-permute-start.2 = (bf16[1,128,1536]{2,1,0:T(8,128)(2,1)}, bf16[1,128,1536]{2,1,0:T(8,128)(2,1)S(1)}, u32[]{:S(2)}, u32[]{:S(2)}) collective-permute-start(bf16[1,128,1536]{2,1,0:T(8,128)(2,1)} %fusion.17), channel_id=1, source_target_pairs={{0,16},{16,32},{32,48},{48,64},{64,80},{80,96},{96,112},{112,128},... | collective-permute-start | bytes 1179656 | tf_op jit(solution)/shard_map/ppermute | solution.py:25
  162.4 115.6 %collective-permute-start.5 = (bf16[1,128,1536]{2,1,0:T(8,128)(2,1)S(1)}, bf16[1,128,1536]{2,1,0:T(8,128)(2,1)S(1)}, u32[]{:S(2)}, u32[]{:S(2)}) collective-permute-start(bf16[1,128,1536]{2,1,0:T(8,128)(2,1)S(1)} %fusion.141), channel_id=1, source_target_pairs={{16,0},{32,16},{48,32},{64,48},{80,64},{96,80},{112,96},{128,112},... | collective-permute-start | bytes 1179656 | tf_op jit(solution)/shard_map/ppermute | solution.py:25
  (16 other events, 111.3 us)
Sparse Core Ops, SparseCore 0:
  9.8 115.9 all-gather.2
  140.5 135.6 all-reduce.1
  278.8 110.2 reduce-scatter.1
where the time goes:
time: 400 us; the launch traced here: 399 us
  waiting for transfers between devices  283 us (71%)
  blocking collectives  31.3 us (8%)
  other arithmetic  27.8 us (7%)
  starting transfers between devices  17.7 us (4%)
  between operations  15.3 us (4%)
  matrix products  13 us (3%)
  local copies, waits for them, and re-layouts  10.5 us (3%)
    reduce_scatter x1, waiting for transfers between devices, per_device(): lax.psum_scatter(lax.optimization_barrier(partial_value.astype(jnp.bfloat...  111 us
    all_gather x1, waiting for transfers between devices, per_device(): lax.all_gather(w_rows, 'tm', axis=0, tiled=True)  86.8 us
    psum x1, waiting for transfers between devices, per_device(): lax.psum(kernel_local.astype(jnp.bfloat16), 'tm').astype(jnp.float32)  78.2 us
    psum x1, blocking collectives, per_device(): lax.psum(gain_local.astype(jnp.bfloat16), 'tm').astype(jnp.float32)  31.3 us
  transfers between devices with their start and end apart: 9, of which 5 were waited for; matrix products, arithmetic and copies ran while one was open for 8% of the time, Pallas kernels for 0%

commit v1 on v0

--- a/solution.py
+++ b/solution.py
@@ -105,7 +105,9 @@
     norm_grad = input_grad * bwd_mask
     gain_local = jnp.sum(norm_grad * saved_hat, axis=0) * factor
     kernel_grad, gain_grad = (
-        lax.psum(kernel_local.astype(jnp.bfloat16), "tm").astype(jnp.float32),
+        jnp.sum(lax.all_gather(kernel_local.astype(jnp.bfloat16), "tm"), axis=0).astype(
+            jnp.float32
+        ),
         lax.psum(gain_local.astype(jnp.bfloat16), "tm").astype(jnp.float32),
     )
     columns = hidden_saved

time: 400 us -> 329 us (0.82)
  waiting for transfers between devices: 283 us -> 213 us
  local copies, waits for them, and re-layouts: 10.5 us -> 6.16 us
    psum x1 -> x0, waiting for transfers between devices: 78.2 us -> none  [per_device(): lax.psum(kernel_local.astype(jnp.bfloat16), 'tm').astype(jnp.float32)]
    all_gather x0 -> x1, waiting for transfers between devices: none -> 72.8 us  [per_device(): lax.all_gather(kernel_local.astype(jnp.bfloat16), 'tm')]
    reduce_scatter x1, waiting for transfers between devices: 111 us -> 50.5 us  [per_device(): lax.psum_scatter(lax.optimization_barrier(partial_value.astype(jnp.bfloat...]
    another operation x32, local copies, waits for them, and re-layouts: 6.1 us -> 0.52 us  [per_device(): jnp.stack([jnp.sum(grad_float * pad_saved[tap_index:tap_index + frames],...]
    all_gather x1, waiting for transfers between devices: 86.8 us -> 82.4 us  [per_device(): lax.all_gather(w_rows, 'tm', axis=0, tiled=True)]
  transfers between devices with their start and end apart: 9 -> 9, of which waited for: 5 -> 5; matrix products, arithmetic and copies ran while one was open for 8% -> 13% of each run, Pallas kernels for 0% -> 0%
where the time goes in v1:
time: 329 us; the launch traced here: 327 us
  waiting for transfers between devices  213 us (65%)
  blocking collectives  34.3 us (10%)
  other arithmetic  27.5 us (8%)
  starting transfers between devices  17.5 us (5%)
  between operations  15.3 us (5%)
  matrix products  12.6 us (4%)
  local copies, waits for them, and re-layouts  6.16 us (2%)
    all_gather x1, waiting for transfers between devices, per_device(): lax.all_gather(w_rows, 'tm', axis=0, tiled=True)  82.4 us
    all_gather x1, waiting for transfers between devices, per_device(): lax.all_gather(kernel_local.astype(jnp.bfloat16), 'tm')  72.8 us
    reduce_scatter x1, waiting for transfers between devices, per_device(): lax.psum_scatter(lax.optimization_barrier(partial_value.astype(jnp.bfloat...  50.5 us
    psum x1, blocking collectives, per_device(): lax.psum(gain_local.astype(jnp.bfloat16), 'tm').astype(jnp.float32)  34.3 us
    ppermute x2, starting transfers between devices, extended(): before = lax.ppermute(last, axis, up)  6.64 us
  transfers between devices with their start and end apart: 9, of which 5 were waited for; matrix products, arithmetic and copies ran while one was open for 13% of the time, Pallas kernels for 0%

profile of v1, /device:TPU:42, one launch (start us, length us, event | category | flops | bytes accessed | tf_op | source)
XLA Modules:
  0.0 326.5 jit_solution(13440001096860377208)
XLA Ops:
  7.2 0.0 copy-start.1
  7.2 0.0 copy-start
  7.2 0.0 all-gather.6.cloned.1.call-start
  7.2 0.7 all-gather.6.cloned.1.call-update
  7.9 0.0 reduce-scatter.2.cloned.1.call-start
  8.0 0.7 reduce.4
  8.7 1.3 fusion.152
  10.0 2.6 fusion.146
  12.6 1.3 compare_convert_fusion
  13.9 0.0 copy-start.69
  13.9 1.1 convert_reduce_fusion.1
  15.0 1.1 convert_reduce_fusion
  16.2 1.2 fusion.52
  17.5 0.3 fusion.73
  17.7 0.4 fusion.56
  18.2 0.1 copy-done.67
  18.3 3.8 %collective-permute-start = (bf16[2,15,1536]{2,1,0:T(8,128)(2,1)S(1)}, bf16[2,15,1536]{2,1,0:T(8,128)(2,1)S(1)}, u32[]{:S(2)}, u32[]{:S(2)}) collective-permute-start(bf16[2,15,1536]{2,1,0:T(8,128)(2,1)S(1)} %get-tuple-element.73), channel_id=1, source_target_pairs={{0,1},{1,2},{2,3},{3,4},{4,5},{5,6},{6,7},{7,8},{8,9},{9,10},{10,1... | collective-permute-start | bytes 276488 | tf_op jit(solution)/shard_map/ppermute | solution.py:16
  22.1 2.0 collective-permute-start.1
  24.1 0.3 slice_reduce_fusion.30
  24.4 0.0 copy-start.5
  24.6 0.2 slice_reduce_fusion.29
  24.9 0.0 copy-start.61
  24.9 0.0 copy-start.63
  24.9 0.8 collective-permute-done
  25.7 5.8 %collective-permute-done.1 = bf16[2,15,1536]{2,1,0:T(8,128)(2,1)S(1)} collective-permute-done((bf16[2,15,1536]{2,1,0:T(8,128)(2,1)S(1)}, bf16[2,15,1536]{2,1,0:T(8,128)(2,1)S(1)}, u32[]{:S(2)}, u32[]{:S(2)}) %collective-permute-start.1) | collective-permute-done | bytes 92192 | tf_op jit(solution)/shard_map/ppermute | solution.py:17
  31.6 0.3 maximum_convert_fusion
  32.0 0.0 copy-start.3
  32.0 6.0 %fusion.20 = f32[2,128,1536]{2,1,0:T(8,128)S(1)} fusion(f32[2,158,1536]{2,1,0:T(8,128)S(1)} %maximum_convert_fusion, f32[1536]{0:T(1024)S(1)} %get-tuple-element.68, f32[1536]{0:T(1024)S(1)} %get-tuple-element.69, f32[1536]{0:T(1024)S(1)} %get-tuple-element.40, f32[1536]{0:T(1024)S(1)} %get-tuple-element.41, f32[1536]{0:T(1024)S(1)} %get-tuple-element.42, ...), kind=kLoop, calls=%fused_computation.43 | loop fusion | flops 23986176 | bytes 50522112 | tf_op jit(solution)/shard_map/add | solution.py:41
  38.2 1.2 copy-done.2
  39.4 3.6 %fusion = bf16[1536,1536]{1,0:T(8,128)(2,1)} fusion(bf16[1,128,1536]{2,1,0:T(8,128)(2,1)S(1)} %copy-done.3, f32[2,128,1536]{2,1,0:T(8,128)S(1)} %fusion.20), kind=kOutput, calls=%fused_computation.1 | convolution fusion | flops 609681408 | bytes 5898240 | tf_op jit(solution)/shard_map/dot_general | solution.py:115
  42.9 0.0 reduce-scatter.2.cloned.1.call-update
  43.0 0.0 all-gather.4.cloned.1.call-start
  43.0 82.4 %all-gather.6.cloned.1.call-done = bf16[1,1536,1536]{2,1,0:T(8,128)(2,1)} async-done(((bf16[1,96,1536]{2,1,0:T(8,128)(2,1)}), bf16[1,1536,1536]{2,1,0:T(8,128)(2,1)}) %all-gather.6.cloned.1.call-update) | async-done | bytes 4718608 | tf_op jit(solution)/shard_map/all_gather | solution.py:74
  125.4 5.4 %fusion.103 = (f32[1536]{0:T(1024)S(1)}, f32[1536]{0:T(1024)S(1)}, f32[1536]{0:T(1024)S(1)}, f32[1536]{0:T(1024)S(1)}, f32[1536]{0:T(1024)S(1)}, /*index=5*/f32[...) fusion(f32[2,158,1536]{2,1,0:T(8,128)S(1)} %maximum_convert_fus, ...), kind=kOutput, calls=%fused_computation.163 | convolution fusion | flops 611037696 | bytes 16594944 | tf_op jit(solution)/shard_map/dot_general | solution.py:77
  130.9 2.0 fusion.104
  133.4 2.8 collective-permute-start.3
  136.2 3.0 collective-permute-start.4
  139.2 0.3 stack.133
  139.5 3.6 %fusion.17 = bf16[1,128,1536]{2,1,0:T(8,128)(2,1)S(1)} fusion(bf16[1,1536,1536]{2,1,0:T(8,128)(2,1)} %all-gather.6.cloned.1.call-done, bf16[1,128,1536]{2,1,0:T(8,128)(2,1)S(1)} %copy-done.1, f32[2,128,1536]{2,1,0:T(8,128)} %copy-done.2), kind=kOutput, calls=%fused_computation.41 | convolution fusion | flops 605552640 | bytes 6291456 | tf_op jit(solution)/shard_map/dot_general | solution.py:72
  143.2 0.0 copy-start.6
  143.5 0.0 copy-start.62
  143.5 0.0 copy-start.64
  143.5 0.0 copy-start.66
  143.5 0.0 copy-start.68
  143.5 0.7 multiply_convert_fusion.4
  144.2 2.1 collective-permute-start.2
  146.3 0.0 all-gather.4.cloned.1.call-update
  146.3 0.0 collective-permute-done.3
  146.3 0.0 collective-permute-done.4
  146.3 0.1 maximum_convert_fusion.1
  146.8 5.1 %fusion.72 = (f32[1536]{0:T(1024)S(1)}, f32[128]{0:T(128)S(1)}, f32[128]{0:T(128)S(1)}, f32[128,1536]{1,0:T(8,128)S(1)}) fusion(bf16[1,128,1536]{2,1,0:T(8,128)(2,1)S(1)} %copy-done, f32[128]{0:T(128)S(1)} %copy-done.68, f32[128]{0:T(128)S(1)} %copy-done.66, f32[1536]{0:T(1024)S(1)} %reduce.4, f32[128]{0:T(128)S(1)} %copy-done.70, ...), kind=kLoop, calls=%fused_computation.132 | loop fusion | flops 13957376 | bytes 25764352 | tf_op jit(solution)/shard_map/reduce_sum | solution.py:106
  151.9 0.4 fusion.141
  152.3 3.6 %collective-permute-start.5 = (bf16[1,128,1536]{2,1,0:T(8,128)(2,1)S(1)}, bf16[1,128,1536]{2,1,0:T(8,128)(2,1)S(1)}, u32[]{:S(2)}, u32[]{:S(2)}) collective-permute-start(bf16[1,128,1536]{2,1,0:T(8,128)(2,1)S(1)} %fusion.141), channel_id=1, source_target_pairs={{16,0},{32,16},{48,32},{64,48},{80,64},{96,80},{112,96},{128,112},... | collective-permute-start | bytes 1179656 | tf_op jit(solution)/shard_map/ppermute | solution.py:25
  156.0 34.3 %psum.7 = bf16[1,1536]{1,0:T(2,128)(2,1)S(1)} all-reduce(bf16[1,1536]{1,0:T(2,128)(2,1)S(1)} %broadcast_in_dim.37), channel_id=1, replica_groups=mesh['section'=16,'tm'=16] {'tm'}, use_global_device_ids=true, to_apply=%region_42.43 | all-reduce | flops 1536 | bytes 6144 | tf_op jit(solution)/shard_map/psum | solution.py:111
  190.3 0.6 broadcast_in_dim.38
  190.9 0.0 collective-permute-done.2
  190.9 0.0 collective-permute-done.5
  190.9 50.5 %reduce-scatter.2.cloned.1.call-done = bf16[96,1536]{1,0:T(8,128)(2,1)} async-done(((bf16[1536,1536]{1,0:T(8,128)(2,1)}), bf16[96,1536]{1,0:T(8,128)(2,1)}) %reduce-scatter.2.cloned.1.call-update) | async-done | bytes 294928 | tf_op jit(solution)/shard_map/reduce_scatter | solution.py:120
  241.4 1.8 bitcast_convert_fusion
  243.2 72.8 %all-gather.4.cloned.1.call-done = bf16[16,31,1536]{2,1,0:T(8,128)(2,1)} async-done(((bf16[1,31,1536]{2,1,0:T(8,128)(2,1)}), bf16[16,31,1536]{2,1,0:T(8,128)(2,1)}) %all-gather.4.cloned.1.call-update) | async-done | bytes 1523728 | tf_op jit(solution)/shard_map/all_gather | solution.py:108
  316.1 1.7 reduce_sum.411
  317.7 0.8 reshape.683
  318.5 0.7 copy.15
  319.3 0.7 copy.16
  (168 shorter events, 0.5 us)
Async XLA Ops:
  7.2 10.6 %copy-start.1 = (bf16[1,128,1536]{2,1,0:T(8,128)(2,1)S(1)}, bf16[1,128,1536]{2,1,0:T(8,128)(2,1)}, u32[]{:S(2)}) copy-start(bf16[1,128,1536]{2,1,0:T(8,128)(2,1)} %param.8) | copy-start | bytes 1179652
  7.2 10.3 %copy-start = (bf16[1,128,1536]{2,1,0:T(8,128)(2,1)S(1)}, bf16[1,128,1536]{2,1,0:T(8,128)(2,1)}, u32[]{:S(2)}) copy-start(bf16[1,128,1536]{2,1,0:T(8,128)(2,1)} %param.9) | copy-start | bytes 1179652
  7.2 118.2 %all-gather.6.cloned.1.call-start = ((), (), s32[]{:S(2)}) async-start(), calls=%async_computation.3 | async-start | bytes 5013504 | tf_op jit(solution)/shard_map/all_gather | solution.py:74
  7.9 233.5 %reduce-scatter.2.cloned.1.call-start = ((), (), s32[]{:S(2)}) async-start(), calls=%async_computation.1 | async-start | bytes 5013504 | tf_op jit(solution)/shard_map/reduce_scatter | solution.py:120
  13.9 4.3 %copy-start.69 = (f32[128]{0:T(128)}, f32[128]{0:T(128)S(1)}, u32[]{:S(2)}) copy-start(f32[128]{0:T(128)S(1)} %get-tuple-element.82) | copy-start | bytes 1540
  17.4 6.7 %copy-start.4 = (f32[1,31,1536]{2,0,1:T(1,128)S(1)}, f32[1,31,1536]{2,0,1:T(1,128)}, u32[]{:S(2)}) copy-start(f32[1,31,1536]{2,0,1:T(1,128)} %param.12) | copy-start | bytes 571396
  18.3 7.5 %collective-permute-start = (bf16[2,15,1536]{2,1,0:T(8,128)(2,1)S(1)}, bf16[2,15,1536]{2,1,0:T(8,128)(2,1)S(1)}, u32[]{:S(2)}, u32[]{:S(2)}) collective-permute-start(bf16[2,15,1536]{2,1,0:T(8,128)(2,1)S(1)} %get-tuple-element.73), channel_id=1, source_target_pairs={{0,1},{1,2},{2,3},{3,4},{4,5},{5,6},{6,7},{7,8},{8,9},{9,10},{10,1... | collective-permute-start | bytes 276488 | tf_op jit(solution)/shard_map/ppermute | solution.py:16
  22.1 9.5 %collective-permute-start.1 = (bf16[2,15,1536]{2,1,0:T(8,128)(2,1)S(1)}, bf16[2,15,1536]{2,1,0:T(8,128)(2,1)S(1)}, u32[]{:S(2)}, u32[]{:S(2)}) collective-permute-start(bf16[2,15,1536]{2,1,0:T(8,128)(2,1)S(1)} %get-tuple-element.74), channel_id=1, source_target_pairs={{1,0},{2,1},{3,2},{4,3},{5,4},{6,5},{7,6},{8,7},{9,8},{10,9},{11,1... | collective-permute-start | bytes 276488 | tf_op jit(solution)/shard_map/ppermute | solution.py:17
  24.4 7.4 %copy-start.5 = (f32[1536]{0:T(1024)}, f32[1536]{0:T(1024)S(1)}, u32[]{:S(2)}) copy-start(f32[1536]{0:T(1024)S(1)} %get-tuple-element.40) | copy-start | bytes 18436
  24.5 7.4 %copy-start.7 = (f32[1536]{0:T(1024)}, f32[1536]{0:T(1024)S(1)}, u32[]{:S(2)}) copy-start(f32[1536]{0:T(1024)S(1)} %get-tuple-element.41) | copy-start | bytes 18436
  24.5 7.4 %copy-start.9 = (f32[1536]{0:T(1024)}, f32[1536]{0:T(1024)S(1)}, u32[]{:S(2)}) copy-start(f32[1536]{0:T(1024)S(1)} %get-tuple-element.42) | copy-start | bytes 18436
  24.5 7.4 %copy-start.11 = (f32[1536]{0:T(1024)}, f32[1536]{0:T(1024)S(1)}, u32[]{:S(2)}) copy-start(f32[1536]{0:T(1024)S(1)} %get-tuple-element.43) | copy-start | bytes 18436
  24.5 7.4 %copy-start.13 = (f32[1536]{0:T(1024)}, f32[1536]{0:T(1024)S(1)}, u32[]{:S(2)}) copy-start(f32[1536]{0:T(1024)S(1)} %get-tuple-element.44) | copy-start | bytes 18436
  24.5 7.4 %copy-start.15 = (f32[1536]{0:T(1024)}, f32[1536]{0:T(1024)S(1)}, u32[]{:S(2)}) copy-start(f32[1536]{0:T(1024)S(1)} %get-tuple-element.45) | copy-start | bytes 18436
  24.5 7.4 %copy-start.17 = (f32[1536]{0:T(1024)}, f32[1536]{0:T(1024)S(1)}, u32[]{:S(2)}) copy-start(f32[1536]{0:T(1024)S(1)} %get-tuple-element.46) | copy-start | bytes 18436
  24.5 7.4 %copy-start.19 = (f32[1536]{0:T(1024)}, f32[1536]{0:T(1024)S(1)}, u32[]{:S(2)}) copy-start(f32[1536]{0:T(1024)S(1)} %get-tuple-element.47) | copy-start | bytes 18436
  24.5 7.4 %copy-start.21 = (f32[1536]{0:T(1024)}, f32[1536]{0:T(1024)S(1)}, u32[]{:S(2)}) copy-start(f32[1536]{0:T(1024)S(1)} %get-tuple-element.48) | copy-start | bytes 18436
  24.5 7.4 %copy-start.23 = (f32[1536]{0:T(1024)}, f32[1536]{0:T(1024)S(1)}, u32[]{:S(2)}) copy-start(f32[1536]{0:T(1024)S(1)} %get-tuple-element.49) | copy-start | bytes 18436
  24.6 7.4 %copy-start.25 = (f32[1536]{0:T(1024)}, f32[1536]{0:T(1024)S(1)}, u32[]{:S(2)}) copy-start(f32[1536]{0:T(1024)S(1)} %get-tuple-element.50) | copy-start | bytes 18436
  24.6 7.4 %copy-start.27 = (f32[1536]{0:T(1024)}, f32[1536]{0:T(1024)S(1)}, u32[]{:S(2)}) copy-start(f32[1536]{0:T(1024)S(1)} %get-tuple-element.51) | copy-start | bytes 18436
  24.6 7.4 %copy-start.29 = (f32[1536]{0:T(1024)}, f32[1536]{0:T(1024)S(1)}, u32[]{:S(2)}) copy-start(f32[1536]{0:T(1024)S(1)} %get-tuple-element.52) | copy-start | bytes 18436
  24.6 7.4 %copy-start.31 = (f32[1536]{0:T(1024)}, f32[1536]{0:T(1024)S(1)}, u32[]{:S(2)}) copy-start(f32[1536]{0:T(1024)S(1)} %get-tuple-element.53) | copy-start | bytes 18436
  24.6 7.4 %copy-start.33 = (f32[1536]{0:T(1024)}, f32[1536]{0:T(1024)S(1)}, u32[]{:S(2)}) copy-start(f32[1536]{0:T(1024)S(1)} %get-tuple-element.54) | copy-start | bytes 18436
  24.6 7.4 %copy-start.35 = (f32[1536]{0:T(1024)}, f32[1536]{0:T(1024)S(1)}, u32[]{:S(2)}) copy-start(f32[1536]{0:T(1024)S(1)} %get-tuple-element.55) | copy-start | bytes 18436
  24.6 7.4 %copy-start.37 = (f32[1536]{0:T(1024)}, f32[1536]{0:T(1024)S(1)}, u32[]{:S(2)}) copy-start(f32[1536]{0:T(1024)S(1)} %get-tuple-element.56) | copy-start | bytes 18436
  24.6 7.4 %copy-start.39 = (f32[1536]{0:T(1024)}, f32[1536]{0:T(1024)S(1)}, u32[]{:S(2)}) copy-start(f32[1536]{0:T(1024)S(1)} %get-tuple-element.57) | copy-start | bytes 18436
  24.8 13.2 %copy-start.41 = (f32[1536]{0:T(1024)}, f32[1536]{0:T(1024)S(1)}, u32[]{:S(2)}) copy-start(f32[1536]{0:T(1024)S(1)} %get-tuple-element.58) | copy-start | bytes 18436
  24.8 13.2 %copy-start.43 = (f32[1536]{0:T(1024)}, f32[1536]{0:T(1024)S(1)}, u32[]{:S(2)}) copy-start(f32[1536]{0:T(1024)S(1)} %get-tuple-element.59) | copy-start | bytes 18436
  24.8 13.2 %copy-start.45 = (f32[1536]{0:T(1024)}, f32[1536]{0:T(1024)S(1)}, u32[]{:S(2)}) copy-start(f32[1536]{0:T(1024)S(1)} %get-tuple-element.60) | copy-start | bytes 18436
  24.9 13.2 %copy-start.47 = (f32[1536]{0:T(1024)}, f32[1536]{0:T(1024)S(1)}, u32[]{:S(2)}) copy-start(f32[1536]{0:T(1024)S(1)} %get-tuple-element.61) | copy-start | bytes 18436
  24.9 13.2 %copy-start.49 = (f32[1536]{0:T(1024)}, f32[1536]{0:T(1024)S(1)}, u32[]{:S(2)}) copy-start(f32[1536]{0:T(1024)S(1)} %get-tuple-element.62) | copy-start | bytes 18436
  24.9 13.2 %copy-start.51 = (f32[1536]{0:T(1024)}, f32[1536]{0:T(1024)S(1)}, u32[]{:S(2)}) copy-start(f32[1536]{0:T(1024)S(1)} %get-tuple-element.63) | copy-start | bytes 18436
  24.9 13.2 %copy-start.53 = (f32[1536]{0:T(1024)}, f32[1536]{0:T(1024)S(1)}, u32[]{:S(2)}) copy-start(f32[1536]{0:T(1024)S(1)} %get-tuple-element.64) | copy-start | bytes 18436
  24.9 13.2 %copy-start.55 = (f32[1536]{0:T(1024)}, f32[1536]{0:T(1024)S(1)}, u32[]{:S(2)}) copy-start(f32[1536]{0:T(1024)S(1)} %get-tuple-element.65) | copy-start | bytes 18436
  24.9 13.2 %copy-start.57 = (f32[1536]{0:T(1024)}, f32[1536]{0:T(1024)S(1)}, u32[]{:S(2)}) copy-start(f32[1536]{0:T(1024)S(1)} %get-tuple-element.66) | copy-start | bytes 18436
  24.9 13.2 %copy-start.59 = (f32[1536]{0:T(1024)}, f32[1536]{0:T(1024)S(1)}, u32[]{:S(2)}) copy-start(f32[1536]{0:T(1024)S(1)} %get-tuple-element.67) | copy-start | bytes 18436
  24.9 13.2 %copy-start.61 = (f32[1536]{0:T(1024)}, f32[1536]{0:T(1024)S(1)}, u32[]{:S(2)}) copy-start(f32[1536]{0:T(1024)S(1)} %get-tuple-element.68) | copy-start | bytes 18436
  24.9 13.2 %copy-start.63 = (f32[1536]{0:T(1024)}, f32[1536]{0:T(1024)S(1)}, u32[]{:S(2)}) copy-start(f32[1536]{0:T(1024)S(1)} %get-tuple-element.69) | copy-start | bytes 18436
  32.0 7.3 %copy-start.3 = (bf16[1,128,1536]{2,1,0:T(8,128)(2,1)S(1)}, bf16[1,128,1536]{2,1,0:T(8,128)(2,1)}, u32[]{:S(2)}) copy-start(bf16[1,128,1536]{2,1,0:T(8,128)(2,1)} %param.10) | copy-start | bytes 1179652
  43.0 273.1 %all-gather.4.cloned.1.call-start = ((), (), s32[]{:S(2)}) async-start(), calls=%async_computation.2 | async-start | bytes 1671168 | tf_op jit(solution)/shard_map/all_gather | solution.py:108
  133.4 12.9 %collective-permute-start.3 = (bf16[15,1536]{1,0:T(8,128)(2,1)S(1)}, bf16[15,1536]{1,0:T(8,128)(2,1)S(1)}, u32[]{:S(2)}, u32[]{:S(2)}) collective-permute-start(bf16[15,1536]{1,0:T(8,128)(2,1)S(1)} %get-tuple-element.75), channel_id=1, source_target_pairs={{0,1},{1,2},{2,3},{3,4},{4,5},{5,6},{6,7},{7,8},{8,9},{9,10},{10,1... | collective-permute-start | bytes 138248 | tf_op jit(solution)/shard_map/ppermute | solution.py:16
  136.2 10.1 %collective-permute-start.4 = (bf16[15,1536]{1,0:T(8,128)(2,1)S(1)}, bf16[15,1536]{1,0:T(8,128)(2,1)S(1)}, u32[]{:S(2)}, u32[]{:S(2)}) collective-permute-start(bf16[15,1536]{1,0:T(8,128)(2,1)S(1)} %get-tuple-element.76), channel_id=1, source_target_pairs={{1,0},{2,1},{3,2},{4,3},{5,4},{6,5},{7,6},{8,7},{9,8},{10,9},{11,1... | collective-permute-start | bytes 138248 | tf_op jit(solution)/shard_map/ppermute | solution.py:17
  143.2 3.3 %copy-start.6 = (f32[1536]{0:T(1024)S(1)}, f32[1536]{0:T(1024)}, u32[]{:S(2)}) copy-start(f32[1536]{0:T(1024)} %copy-done.5) | copy-start | bytes 18436
  143.2 3.3 %copy-start.8 = (f32[1536]{0:T(1024)S(1)}, f32[1536]{0:T(1024)}, u32[]{:S(2)}) copy-start(f32[1536]{0:T(1024)} %copy-done.7) | copy-start | bytes 18436
  143.2 3.3 %copy-start.10 = (f32[1536]{0:T(1024)S(1)}, f32[1536]{0:T(1024)}, u32[]{:S(2)}) copy-start(f32[1536]{0:T(1024)} %copy-done.9) | copy-start | bytes 18436
  143.2 3.3 %copy-start.12 = (f32[1536]{0:T(1024)S(1)}, f32[1536]{0:T(1024)}, u32[]{:S(2)}) copy-start(f32[1536]{0:T(1024)} %copy-done.11) | copy-start | bytes 18436
  143.2 3.3 %copy-start.14 = (f32[1536]{0:T(1024)S(1)}, f32[1536]{0:T(1024)}, u32[]{:S(2)}) copy-start(f32[1536]{0:T(1024)} %copy-done.13) | copy-start | bytes 18436
  143.2 3.3 %copy-start.16 = (f32[1536]{0:T(1024)S(1)}, f32[1536]{0:T(1024)}, u32[]{:S(2)}) copy-start(f32[1536]{0:T(1024)} %copy-done.15) | copy-start | bytes 18436
  143.2 3.3 %copy-start.18 = (f32[1536]{0:T(1024)S(1)}, f32[1536]{0:T(1024)}, u32[]{:S(2)}) copy-start(f32[1536]{0:T(1024)} %copy-done.17) | copy-start | bytes 18436
  143.2 3.3 %copy-start.20 = (f32[1536]{0:T(1024)S(1)}, f32[1536]{0:T(1024)}, u32[]{:S(2)}) copy-start(f32[1536]{0:T(1024)} %copy-done.19) | copy-start | bytes 18436
  143.3 3.3 %copy-start.22 = (f32[1536]{0:T(1024)S(1)}, f32[1536]{0:T(1024)}, u32[]{:S(2)}) copy-start(f32[1536]{0:T(1024)} %copy-done.21) | copy-start | bytes 18436
  143.3 3.3 %copy-start.24 = (f32[1536]{0:T(1024)S(1)}, f32[1536]{0:T(1024)}, u32[]{:S(2)}) copy-start(f32[1536]{0:T(1024)} %copy-done.23) | copy-start | bytes 18436
  143.3 3.3 %copy-start.26 = (f32[1536]{0:T(1024)S(1)}, f32[1536]{0:T(1024)}, u32[]{:S(2)}) copy-start(f32[1536]{0:T(1024)} %copy-done.25) | copy-start | bytes 18436
  143.3 3.3 %copy-start.28 = (f32[1536]{0:T(1024)S(1)}, f32[1536]{0:T(1024)}, u32[]{:S(2)}) copy-start(f32[1536]{0:T(1024)} %copy-done.27) | copy-start | bytes 18436
  143.3 3.3 %copy-start.30 = (f32[1536]{0:T(1024)S(1)}, f32[1536]{0:T(1024)}, u32[]{:S(2)}) copy-start(f32[1536]{0:T(1024)} %copy-done.29) | copy-start | bytes 18436
  143.3 3.3 %copy-start.32 = (f32[1536]{0:T(1024)S(1)}, f32[1536]{0:T(1024)}, u32[]{:S(2)}) copy-start(f32[1536]{0:T(1024)} %copy-done.31) | copy-start | bytes 18436
  143.3 3.3 %copy-start.34 = (f32[1536]{0:T(1024)S(1)}, f32[1536]{0:T(1024)}, u32[]{:S(2)}) copy-start(f32[1536]{0:T(1024)} %copy-done.33) | copy-start | bytes 18436
  143.3 3.3 %copy-start.36 = (f32[1536]{0:T(1024)S(1)}, f32[1536]{0:T(1024)}, u32[]{:S(2)}) copy-start(f32[1536]{0:T(1024)} %copy-done.35) | copy-start | bytes 18436
  143.3 3.3 %copy-start.38 = (f32[1536]{0:T(1024)S(1)}, f32[1536]{0:T(1024)}, u32[]{:S(2)}) copy-start(f32[1536]{0:T(1024)} %copy-done.37) | copy-start | bytes 18436
  143.3 3.3 %copy-start.40 = (f32[1536]{0:T(1024)S(1)}, f32[1536]{0:T(1024)}, u32[]{:S(2)}) copy-start(f32[1536]{0:T(1024)} %copy-done.39) | copy-start | bytes 18436
  143.4 3.3 %copy-start.42 = (f32[1536]{0:T(1024)S(1)}, f32[1536]{0:T(1024)}, u32[]{:S(2)}) copy-start(f32[1536]{0:T(1024)} %copy-done.41) | copy-start | bytes 18436
  143.4 3.3 %copy-start.44 = (f32[1536]{0:T(1024)S(1)}, f32[1536]{0:T(1024)}, u32[]{:S(2)}) copy-start(f32[1536]{0:T(1024)} %copy-done.43) | copy-start | bytes 18436
  144.2 46.7 %collective-permute-start.2 = (bf16[1,128,1536]{2,1,0:T(8,128)(2,1)S(1)}, bf16[1,128,1536]{2,1,0:T(8,128)(2,1)S(1)}, u32[]{:S(2)}, u32[]{:S(2)}) collective-permute-start(bf16[1,128,1536]{2,1,0:T(8,128)(2,1)S(1)} %fusion.17), channel_id=1, source_target_pairs={{0,16},{16,32},{32,48},{48,64},{64,80},{80,96},{96,112},{112,128},... | collective-permute-start | bytes 1179656 | tf_op jit(solution)/shard_map/ppermute | solution.py:25
  152.3 38.6 %collective-permute-start.5 = (bf16[1,128,1536]{2,1,0:T(8,128)(2,1)S(1)}, bf16[1,128,1536]{2,1,0:T(8,128)(2,1)S(1)}, u32[]{:S(2)}, u32[]{:S(2)}) collective-permute-start(bf16[1,128,1536]{2,1,0:T(8,128)(2,1)S(1)} %fusion.141), channel_id=1, source_target_pairs={{16,0},{32,16},{48,32},{64,48},{80,64},{96,80},{112,96},{128,112},... | collective-permute-start | bytes 1179656 | tf_op jit(solution)/shard_map/ppermute | solution.py:25
  (16 other events, 45.0 us)
Sparse Core Ops, SparseCore 0:
  9.8 115.5 all-gather.5
  128.0 113.3 reduce-scatter.1
  243.8 72.2 all-gather.3
